TPU v7x, 32 devices: a whole 2x2x4 slice. The times are simulated.
32 devices in a mesh: gz: 8 (over z, core), xy: 4 (over y, x).
Axes of the slice: x: 2, y: 2, z: 4, core: 2. Of those that a mesh axis runs over, the one named last changes fastest.
Arguments:
- slab_image: float32 [32, 128, 1024], P('gz', None, 'xy'), may hold values from 0 to 1
- width_taps: float32 [16, 5], replicated, may hold values from -2.5 to 2.5
- height_taps: float32 [16, 5], replicated, may hold values from -2.5 to 2.5
- depth_taps: float32 [16, 5], replicated, may hold values from -2.5 to 2.5
- fragment_ids: int32 [32, 128, 1024], P(None, 'gz', 'xy'), may hold values from 0 to 1023, as said below
- fragment_owner: int32 [32768, 1], P(('gz', 'xy')), may hold values from 0 to 3, as said below
- coarse_centroids: float32 [16, 1024], P(None, ('gz', 'xy')), may hold values from -24 to 24
- parent_map: int32 [4096], P(('gz', 'xy')), may hold values from 0 to 31
- fine_offsets: float32 [16, 4096], P(None, ('gz', 'xy')), may hold values from -2.5 to 2.5
Outputs:
- fragment_means: float32 [16, 32768], P(None, ('gz', 'xy'))
- centroids: float32 [16, 4096], P(None, ('gz', 'xy'))
Inputs may be any that keep to these rules, and one draw needn't show every extreme that they name: `fragment_ids`: ids are local to a pencil block of 32 x 16 x 256 voxels; every id 0 to 1023 occurs in every block. `fragment_owner`: of the 1024 fragments of one pencil block at most 512 name the same owner; in each row along xy some owner takes exactly 512 from every block of that row.
All inputs are finite; a program needn't handle non-finite values.
Results may differ from a plain program's by a relative error of at most 0.00038.
Values may be sent and summed in bfloat16 or wider, within the bound.
A program may use at most 128 MiB of HBM per device.

v0:
```python
import jax
import jax.numpy as jnp
from jax import lax
from jax.sharding import PartitionSpec as P

TAPS = 5
BZ = 4
ITERS = 3


HIGH = lax.Precision.HIGHEST
sharpness = 2.0
group_span = 4


def with_halo(cells, sides, width):
    for axis, dim in sides:
        count = lax.axis_size(axis)
        ends = count - 1
        head = lax.slice_in_dim(cells, 0, width, axis=dim)
        tail = lax.slice_in_dim(cells, cells.shape[dim] - width, cells.shape[dim], axis=dim)
        cells = jnp.concatenate(
            [
                lax.ppermute(tail, axis, [(i, (i + 1) % count) for i in range(ends)]),
                cells,
                lax.ppermute(head, axis, [((i + 1) % count, i) for i in range(ends)]),
            ],
            axis=dim,
        )
    return cells


def planar_filter(padded, width_taps, height_taps):
    reach = width_taps.shape[1]
    rows = padded.shape[1] - reach + 1
    cols = padded.shape[2] - reach + 1
    pieces = []
    for chan_start in range(0, width_taps.shape[0], group_span):
        width_tap = width_taps[chan_start : chan_start + group_span][:, :, None, None, None]
        height_tap = height_taps[chan_start : chan_start + group_span][:, :, None, None, None]
        across = width_tap[:, 0] * padded[None, :, :, 0:cols]
        for tap_shift in range(1, reach):
            across = (
                across + width_tap[:, tap_shift] * padded[None, :, :, tap_shift : tap_shift + cols]
            )
        planar = height_tap[:, 0] * across[:, :, 0:rows, :]
        for tap_shift in range(1, reach):
            planar = (
                planar + height_tap[:, tap_shift] * across[:, :, tap_shift : tap_shift + rows, :]
            )
        pieces.append(planar.astype(jnp.bfloat16))
    return jnp.concatenate(pieces, axis=0)


def depth_filter(planar, depth_taps):
    reach = depth_taps.shape[1]
    half = reach // 2
    depth = planar.shape[1]
    planar = lax.optimization_barrier(planar)
    pieces = []
    for chan_start in range(0, planar.shape[0], group_span):
        block = planar[chan_start : chan_start + group_span].astype(jnp.float32)
        padded = jnp.pad(block, ((0, 0), (half, half), (0, 0), (0, 0)))
        depth_tap = depth_taps[chan_start : chan_start + group_span][:, :, None, None, None]
        response = depth_tap[:, 0] * padded[:, 0:depth]
        for tap_shift in range(1, reach):
            response = response + depth_tap[:, tap_shift] * padded[:, tap_shift : tap_shift + depth]
        pieces.append(jnp.tanh(response).astype(jnp.bfloat16))
    return jnp.concatenate(pieces, axis=0)


def fragment_sums(features, fragment_ids, fragments):
    chans, depth, rows, cols = features.shape
    labels = jnp.arange(fragments, dtype=jnp.int32)
    voxels = BZ * rows * cols

    def add_block(index, carry):
        sums, counts = carry
        start = index * BZ
        block = lax.dynamic_slice_in_dim(features, start, BZ, 1).reshape(chans, voxels)
        block_ids = lax.dynamic_slice_in_dim(fragment_ids, start, BZ, 0).reshape(voxels)
        member = block_ids[:, None] == labels[None, :]
        sums = sums + jnp.dot(
            block, member.astype(jnp.bfloat16), preferred_element_type=jnp.float32
        )
        counts = counts + jnp.sum(member.astype(jnp.float32), axis=0)
        return (sums, counts)

    start_carry = (jnp.zeros((chans, fragments), jnp.float32), jnp.zeros((fragments,), jnp.float32))
    return lax.fori_loop(0, depth // BZ, add_block, start_carry)


def soft_stats(frags, weight, cents):
    cross = lax.dot_general(
        frags, cents, (((0,), (0,)), ((), ())), precision=HIGH, preferred_element_type=jnp.float32
    )
    distance = (
        jnp.sum(frags * frags, axis=0)[:, None]
        + jnp.sum(cents * cents, axis=0)[None, :]
        - 2.0 * cross
    )
    scores = -sharpness * distance
    top = jnp.max(scores, axis=1, keepdims=True)
    expo = jnp.exp(scores - top)
    resp = expo / jnp.sum(expo, axis=1, keepdims=True)
    numer = jnp.dot(
        frags * weight[None, :], resp, precision=HIGH, preferred_element_type=jnp.float32
    )
    denom = jnp.dot(weight[None, :], resp, precision=HIGH, preferred_element_type=jnp.float32)
    return (numer, denom)


def shards(
    slab_image,
    width_taps,
    height_taps,
    depth_taps,
    fragment_ids,
    fragment_owner,
    coarse_centroids,
    parent_map,
    fine_offsets,
):
    half = TAPS // 2
    rimmed = with_halo(slab_image, (("xy", 2),), TAPS // 2)
    rimmed = jnp.pad(rimmed, ((0, 0), (half, half), (0, 0)))
    planar = planar_filter(rimmed, width_taps, height_taps)
    planar = lax.all_to_all(planar, "gz", split_axis=2, concat_axis=1, tiled=True)
    features = depth_filter(planar, depth_taps)
    fragments = fragment_owner.shape[0]
    sums, counts = fragment_sums(features, fragment_ids, fragments)
    means = sums / counts[None, :]
    coarse_count = coarse_centroids.shape[1]
    select = (parent_map[None, :] == jnp.arange(coarse_count, dtype=jnp.int32)[:, None]).astype(
        jnp.float32
    )
    centroids = (
        jnp.dot(coarse_centroids, select, precision=HIGH, preferred_element_type=jnp.float32)
        + fine_offsets
    )
    fine_count = centroids.shape[1]
    pseudo = float(fragment_ids.size // fine_count)
    owner = fragment_owner[:, 0]
    lanes = lax.axis_size("xy")
    capacity = min(fragments // 2, 4 * fragments // lanes)
    pick = (owner[:, None] == jnp.arange(lanes, dtype=jnp.int32)[None, :]).astype(jnp.int32)
    rank = jnp.sum((jnp.cumsum(pick, axis=0) - 1) * pick, axis=1)
    slot = owner * capacity + rank
    packed = jnp.zeros((means.shape[0], lanes * capacity), jnp.float32).at[:, slot].set(means)
    weights = jnp.zeros((1, lanes * capacity), jnp.float32).at[0, slot].set(counts)
    arrived, arrived_weight = (
        lax.all_to_all(packed, "xy", split_axis=1, concat_axis=1, tiled=True),
        lax.all_to_all(weights, "xy", split_axis=1, concat_axis=1, tiled=True),
    )
    for step in range(ITERS):
        numer, denom = soft_stats(arrived, arrived_weight[0], centroids)
        centroids = (numer + pseudo * centroids) / (denom + pseudo)
    return (means, centroids)


def solution(mesh):
    placed = (
        P("gz", None, "xy"),
        P(),
        P(),
        P(),
        P(None, "gz", "xy"),
        P(("gz", "xy"), None),
        P(None, ("gz", "xy")),
        P(("gz", "xy")),
        P(None, ("gz", "xy")),
    )
    return jax.shard_map(
        shards,
        mesh=mesh,
        in_specs=placed,
        out_specs=(P(None, ("gz", "xy")), P(None, ("gz", "xy"))),
        check_vma=False,
    )
```

profile of v0, /device:TPU:0, one launch (start us, length us, event | category | flops | bytes accessed | tf_op | source)
XLA Modules:
  0.0 379.4 jit_solution(12561259763467322268)
XLA Ops:
  0.6 1.2 fusion.109
  1.8 4.9 %collective-permute-start = (f32[4,128,2]{2,1,0:T(8,128)S(1)}, f32[4,128,2]{2,1,0:T(8,128)S(1)}, u32[]{:S(2)}, u32[]{:S(2)}) collective-permute-start(f32[4,128,2]{2,1,0:T(8,128)S(1)} %get-tuple-element.217), channel_id=1, source_target_pairs={{0,1},{1,2},{2,3},{4,5},{5,6},{6,7},{8,9},{9,10},{10,11},{12,13},{... | collective-permute-start | bytes 12296 | tf_op jit(solution)/shard_map/ppermute | solution.py:24
  6.7 1.3 collective-permute-start.1
  8.0 0.9 fusion.112
  9.1 0.9 fusion.111
  12.2 7.6 %collective-permute-done.1 = f32[4,128,2]{2,1,0:T(8,128)S(1)} collective-permute-done((f32[4,128,2]{2,1,0:T(8,128)S(1)}, f32[4,128,2]{2,1,0:T(8,128)S(1)}, u32[]{:S(2)}, u32[]{:S(2)}) %collective-permute-start.1) | collective-permute-done | bytes 4128 | tf_op jit(solution)/shard_map/ppermute | solution.py:26
  19.8 1.4 select_maximum_fusion
  22.9 2.9 multiply_add_fusion.3
  25.8 2.8 fusion.69
  28.6 2.8 fusion.64
  31.4 2.7 multiply_add_fusion.1
  34.1 2.8 fusion.59
  36.9 2.8 fusion.54
  39.7 4.3 %pad_maximum_fusion = bf16[16,4,128,256]{3,1,0,2:T(4,128)(2,1)} fusion(bf16[4,4,128,256]{3,1,0,2:T(4,128)(2,1)S(1)} %fusion.54, bf16[4,4,128,256]{3,1,0,2:T(4,128)(2,1)S(1)} %fusion.59, bf16[4,4,128,256]{3,1,0,2:T(4,128)(2,1)S(1)} %fusion.64, bf16[4,4,128,256]{3,1,0,2:T(4,128)(2,1)S(1)} %fusion.69), kind=kLoop, calls=%fused_computation.12 | loop fusion | flops 6291456 | bytes 8388608 | tf_op jit(solution)/shard_map/concatenate | solution.py:52
  44.1 5.0 %all-to-all-start = ((bf16[16,4,128,256]{3,1,0,2:T(4,128)(2,1)}), bf16[16,4,128,256]{3,1,0,2:T(4,128)(2,1)}, u32[]{:S(2)}, u32[]{:S(2)}) async-start(bf16[16,4,128,256]{3,1,0,2:T(4,128)(2,1)} %pad_maximum_fusion), calls=%async_computation | async-start | bytes 8388608 | tf_op jit(solution)/shard_map/all_to_all | solution.py:128
  49.6 1.1 reduce-window.6
  52.5 90.7 %all-to-all-done = bf16[16,4,128,256]{3,1,0,2:T(4,128)(2,1)} async-done(((bf16[16,4,128,256]{3,1,0,2:T(4,128)(2,1)}), bf16[16,4,128,256]{3,1,0,2:T(4,128)(2,1)}, u32[]{:S(2)}, u32[]{:S(2)}) %all-to-all-start) | async-done | bytes 4194336 | tf_op jit(solution)/shard_map/all_to_all | solution.py:128
  143.2 4.6 %copy.108 = bf16[16,4,128,256]{3,2,1,0:T(8,128)(2,1)S(1)} copy(bf16[16,4,128,256]{3,1,0,2:T(4,128)(2,1)} %all-to-all-done) | data formatting | bytes 8388608 | tf_op jit(solution)/shard_map/all_to_all | solution.py:128
  148.4 1.2 slice_convert_fusion.3
  152.8 2.3 pad_maximum_fusion.1
  155.0 193.2 %while.16 = (s32[]{:T(128)}, f32[16,1024]{1,0:T(8,128)S(1)}, f32[1024]{0:T(1024)S(1)}, bf16[16,32,16,256]{3,2,1,0:T(8,128)(2,1)}, s32[32,16,256]{2,1,0:T(8,128)}...) while((s32[]{:T(128)}, f32[16,1024]{1,0:T(8,128)S(1)}, f32[1024]{0:T(1024)S(1)}, ...), condition=%wide.region_2.3_spmd.clone, body=%wide.region_0.2_spmd.clone.sunk | while | flops 604013568 | bytes 3162270 | solution.py:90
  155.9 1.1 constant_dynamic-slice_fusion.4
  157.3 14.0 %fusion.132 = f32[16,1024]{1,0:T(8,128)S(1)} fusion(bf16[16,16384]{1,0:T(8,128)(2,1)S(1)} %bitcast.93, s32[16384]{0:T(1024)S(1)} %bitcast.96, f32[16,1024]{1,0:T(8,128)S(1)} %get-tuple-element.294, pred[]{:T(512)S(6)} %compare.27), kind=kOutput, calls=%fused_computation.8.clone.1 | convolution fusion | flops 553680896 | bytes 720897 | tf_op jit(solution)/shard_map/while/body/eval_jaxpr/dot_general | solution.py:83
  171.3 7.8 %fusion.133 = f32[1024]{0:T(1024)S(1)} fusion(s32[16384]{0:T(1024)S(1)} %bitcast.97), kind=kLoop, calls=%fused_computation.6.clone.1 | loop fusion | flops 50330624 | bytes 69632 | tf_op jit(solution)/shard_map/while/body/eval_jaxpr/reduce_sum | solution.py:86
  179.2 0.8 constant_dynamic-slice_fusion.5
  180.1 1.1 constant_dynamic-slice_fusion.4
  181.5 14.0 %fusion.132 = f32[16,1024]{1,0:T(8,128)S(1)} fusion(bf16[16,16384]{1,0:T(8,128)(2,1)S(1)} %bitcast.93, s32[16384]{0:T(1024)S(1)} %bitcast.96, f32[16,1024]{1,0:T(8,128)S(1)} %get-tuple-element.294, pred[]{:T(512)S(6)} %compare.27), kind=kOutput, calls=%fused_computation.8.clone.1 | convolution fusion | flops 553680896 | bytes 720897 | tf_op jit(solution)/shard_map/while/body/eval_jaxpr/dot_general | solution.py:83
  195.5 7.8 %fusion.133 = f32[1024]{0:T(1024)S(1)} fusion(s32[16384]{0:T(1024)S(1)} %bitcast.97), kind=kLoop, calls=%fused_computation.6.clone.1 | loop fusion | flops 50330624 | bytes 69632 | tf_op jit(solution)/shard_map/while/body/eval_jaxpr/reduce_sum | solution.py:86
  203.3 0.8 constant_dynamic-slice_fusion.5
  204.2 1.1 constant_dynamic-slice_fusion.4
  205.6 14.0 %fusion.132 = f32[16,1024]{1,0:T(8,128)S(1)} fusion(bf16[16,16384]{1,0:T(8,128)(2,1)S(1)} %bitcast.93, s32[16384]{0:T(1024)S(1)} %bitcast.96, f32[16,1024]{1,0:T(8,128)S(1)} %get-tuple-element.294, pred[]{:T(512)S(6)} %compare.27), kind=kOutput, calls=%fused_computation.8.clone.1 | convolution fusion | flops 553680896 | bytes 720897 | tf_op jit(solution)/shard_map/while/body/eval_jaxpr/dot_general | solution.py:83
  219.6 7.8 %fusion.133 = f32[1024]{0:T(1024)S(1)} fusion(s32[16384]{0:T(1024)S(1)} %bitcast.97), kind=kLoop, calls=%fused_computation.6.clone.1 | loop fusion | flops 50330624 | bytes 69632 | tf_op jit(solution)/shard_map/while/body/eval_jaxpr/reduce_sum | solution.py:86
  227.5 0.8 constant_dynamic-slice_fusion.5
  228.4 1.1 constant_dynamic-slice_fusion.4
  229.8 14.0 %fusion.132 = f32[16,1024]{1,0:T(8,128)S(1)} fusion(bf16[16,16384]{1,0:T(8,128)(2,1)S(1)} %bitcast.93, s32[16384]{0:T(1024)S(1)} %bitcast.96, f32[16,1024]{1,0:T(8,128)S(1)} %get-tuple-element.294, pred[]{:T(512)S(6)} %compare.27), kind=kOutput, calls=%fused_computation.8.clone.1 | convolution fusion | flops 553680896 | bytes 720897 | tf_op jit(solution)/shard_map/while/body/eval_jaxpr/dot_general | solution.py:83
  243.8 7.8 %fusion.133 = f32[1024]{0:T(1024)S(1)} fusion(s32[16384]{0:T(1024)S(1)} %bitcast.97), kind=kLoop, calls=%fused_computation.6.clone.1 | loop fusion | flops 50330624 | bytes 69632 | tf_op jit(solution)/shard_map/while/body/eval_jaxpr/reduce_sum | solution.py:86
  251.6 0.8 constant_dynamic-slice_fusion.5
  252.5 1.1 constant_dynamic-slice_fusion.4
  253.9 14.0 %fusion.132 = f32[16,1024]{1,0:T(8,128)S(1)} fusion(bf16[16,16384]{1,0:T(8,128)(2,1)S(1)} %bitcast.93, s32[16384]{0:T(1024)S(1)} %bitcast.96, f32[16,1024]{1,0:T(8,128)S(1)} %get-tuple-element.294, pred[]{:T(512)S(6)} %compare.27), kind=kOutput, calls=%fused_computation.8.clone.1 | convolution fusion | flops 553680896 | bytes 720897 | tf_op jit(solution)/shard_map/while/body/eval_jaxpr/dot_general | solution.py:83
  267.9 7.8 %fusion.133 = f32[1024]{0:T(1024)S(1)} fusion(s32[16384]{0:T(1024)S(1)} %bitcast.97), kind=kLoop, calls=%fused_computation.6.clone.1 | loop fusion | flops 50330624 | bytes 69632 | tf_op jit(solution)/shard_map/while/body/eval_jaxpr/reduce_sum | solution.py:86
  276.7 1.1 constant_dynamic-slice_fusion.4
  278.1 14.0 %fusion.132 = f32[16,1024]{1,0:T(8,128)S(1)} fusion(bf16[16,16384]{1,0:T(8,128)(2,1)S(1)} %bitcast.93, s32[16384]{0:T(1024)S(1)} %bitcast.96, f32[16,1024]{1,0:T(8,128)S(1)} %get-tuple-element.294, pred[]{:T(512)S(6)} %compare.27), kind=kOutput, calls=%fused_computation.8.clone.1 | convolution fusion | flops 553680896 | bytes 720897 | tf_op jit(solution)/shard_map/while/body/eval_jaxpr/dot_general | solution.py:83
  292.1 7.8 %fusion.133 = f32[1024]{0:T(1024)S(1)} fusion(s32[16384]{0:T(1024)S(1)} %bitcast.97), kind=kLoop, calls=%fused_computation.6.clone.1 | loop fusion | flops 50330624 | bytes 69632 | tf_op jit(solution)/shard_map/while/body/eval_jaxpr/reduce_sum | solution.py:86
  300.8 1.1 constant_dynamic-slice_fusion.4
  302.2 14.0 %fusion.132 = f32[16,1024]{1,0:T(8,128)S(1)} fusion(bf16[16,16384]{1,0:T(8,128)(2,1)S(1)} %bitcast.93, s32[16384]{0:T(1024)S(1)} %bitcast.96, f32[16,1024]{1,0:T(8,128)S(1)} %get-tuple-element.294, pred[]{:T(512)S(6)} %compare.27), kind=kOutput, calls=%fused_computation.8.clone.1 | convolution fusion | flops 553680896 | bytes 720897 | tf_op jit(solution)/shard_map/while/body/eval_jaxpr/dot_general | solution.py:83
  316.2 7.8 %fusion.133 = f32[1024]{0:T(1024)S(1)} fusion(s32[16384]{0:T(1024)S(1)} %bitcast.97), kind=kLoop, calls=%fused_computation.6.clone.1 | loop fusion | flops 50330624 | bytes 69632 | tf_op jit(solution)/shard_map/while/body/eval_jaxpr/reduce_sum | solution.py:86
  325.0 1.1 constant_dynamic-slice_fusion.4
  326.4 14.0 %fusion.132 = f32[16,1024]{1,0:T(8,128)S(1)} fusion(bf16[16,16384]{1,0:T(8,128)(2,1)S(1)} %bitcast.93, s32[16384]{0:T(1024)S(1)} %bitcast.96, f32[16,1024]{1,0:T(8,128)S(1)} %get-tuple-element.294, pred[]{:T(512)S(6)} %compare.27), kind=kOutput, calls=%fused_computation.8.clone.1 | convolution fusion | flops 553680896 | bytes 720897 | tf_op jit(solution)/shard_map/while/body/eval_jaxpr/dot_general | solution.py:83
  340.4 7.8 %fusion.133 = f32[1024]{0:T(1024)S(1)} fusion(s32[16384]{0:T(1024)S(1)} %bitcast.97), kind=kLoop, calls=%fused_computation.6.clone.1 | loop fusion | flops 50330624 | bytes 69632 | tf_op jit(solution)/shard_map/while/body/eval_jaxpr/reduce_sum | solution.py:86
  348.4 3.3 scatter_custom_fusion
  351.8 0.9 copy.114
  352.7 3.6 all-to-all-start.1
  357.0 4.9 %scatter_custom_fusion.1 = f32[2048]{0:T(1024)} fusion(s32[1024]{0:T(1024)S(1)} %broadcast_select_fusion, f32[1024]{0:T(1024)S(1)} %get-tuple-element.113, f32[]{:T(128)} %constant.57.clone.1), kind=kCustom, calls=%fused_computation.182 | custom fusion | bytes 8196
  361.8 3.9 %all-to-all-start.2 = ((f32[1,4,512]{2,0,1:T(1,128)}), f32[1,4,512]{2,0,1:T(1,128)S(1)}, u32[]{:S(2)}, u32[]{:S(2)}) async-start(f32[1,4,512]{2,0,1:T(1,128)} %bitcast.22), calls=%async_computation.2 | async-start | bytes 16384 | tf_op jit(solution)/shard_map/all_to_all | solution.py:153
  365.8 1.2 fusion.113
  367.1 3.3 all-to-all-done.2
  370.4 0.9 fusion.77
  371.3 1.0 multiply_reduce_fusion.2
  372.3 1.2 fusion.114
  373.7 0.9 fusion.78
  374.6 1.0 multiply_reduce_fusion.1
  375.6 1.2 fusion.115
  376.9 0.9 fusion.79
  377.9 1.6 fusion.73
  (99 shorter events, 17.5 us)
Async XLA Ops:
  0.6 51.7 %copy-start = (f32[16,32]{1,0:T(8,128)S(1)}, f32[16,32]{1,0:T(8,128)}, u32[]{:S(2)}) copy-start(f32[16,32]{1,0:T(8,128)} %param.17) | copy-start | bytes 6148
  1.8 10.4 %collective-permute-start = (f32[4,128,2]{2,1,0:T(8,128)S(1)}, f32[4,128,2]{2,1,0:T(8,128)S(1)}, u32[]{:S(2)}, u32[]{:S(2)}) collective-permute-start(f32[4,128,2]{2,1,0:T(8,128)S(1)} %get-tuple-element.217), channel_id=1, source_target_pairs={{0,1},{1,2},{2,3},{4,5},{5,6},{6,7},{8,9},{9,10},{10,11},{12,13},{... | collective-permute-start | bytes 12296 | tf_op jit(solution)/shard_map/ppermute | solution.py:24
  6.7 13.1 %collective-permute-start.1 = (f32[4,128,2]{2,1,0:T(8,128)S(1)}, f32[4,128,2]{2,1,0:T(8,128)S(1)}, u32[]{:S(2)}, u32[]{:S(2)}) collective-permute-start(f32[4,128,2]{2,1,0:T(8,128)S(1)} %get-tuple-element.218), channel_id=1, source_target_pairs={{1,0},{2,1},{3,2},{5,4},{6,5},{7,6},{9,8},{10,9},{11,10},{13,12},{... | collective-permute-start | bytes 12296 | tf_op jit(solution)/shard_map/ppermute | solution.py:26
  44.1 5.1 %copy-start.1 = (f32[16,5]{0,1:T(8,128)S(1)}, f32[16,5]{0,1:T(8,128)}, u32[]{:S(2)}) copy-start(f32[16,5]{0,1:T(8,128)} %param.14) | copy-start | bytes 964
  44.1 5.5 %copy-start.2 = (s32[1024,1]{0,1:T(1,128)S(1)}, s32[1024,1]{0,1:T(1,128)}, u32[]{:S(2)}) copy-start(s32[1024,1]{0,1:T(1,128)} %param.16) | copy-start | bytes 12292
  44.1 8.1 %copy-start.5 = (s32[2]{0:T(128)S(1)}, s32[2]{0:T(128)}, u32[]{:S(2)}) copy-start(s32[2]{0:T(128)} %constant.78) | copy-start | bytes 28
  44.1 8.2 %copy-start.6 = (s32[2]{0:T(128)S(1)}, s32[2]{0:T(128)}, u32[]{:S(2)}) copy-start(s32[2]{0:T(128)} %constant.81) | copy-start | bytes 28
  44.1 8.3 %copy-start.3 = (f32[16,128]{1,0:T(8,128)S(1)}, f32[16,128]{1,0:T(8,128)}, u32[]{:S(2)}) copy-start(f32[16,128]{1,0:T(8,128)} %param.19) | copy-start | bytes 24580
  44.1 8.3 %copy-start.4 = (s32[128]{0:T(128)S(1)}, s32[128]{0:T(128)}, u32[]{:S(2)}) copy-start(s32[128]{0:T(128)} %param.18) | copy-start | bytes 1540
  44.1 99.1 %all-to-all-start = ((bf16[16,4,128,256]{3,1,0,2:T(4,128)(2,1)}), bf16[16,4,128,256]{3,1,0,2:T(4,128)(2,1)}, u32[]{:S(2)}, u32[]{:S(2)}) async-start(bf16[16,4,128,256]{3,1,0,2:T(4,128)(2,1)} %pad_maximum_fusion), calls=%async_computation | async-start | bytes 8388608 | tf_op jit(solution)/shard_map/all_to_all | solution.py:128
  352.7 9.1 %all-to-all-start.1 = ((f32[16,4,512]{2,0,1:T(8,128)}), f32[16,4,512]{2,0,1:T(8,128)S(1)}, u32[]{:S(2)}, u32[]{:S(2)}) async-start(f32[16,4,512]{2,0,1:T(8,128)} %copy.114), calls=%async_computation.1 | async-start | bytes 262144 | tf_op jit(solution)/shard_map/all_to_all | solution.py:152
  361.8 8.6 %all-to-all-start.2 = ((f32[1,4,512]{2,0,1:T(1,128)}), f32[1,4,512]{2,0,1:T(1,128)S(1)}, u32[]{:S(2)}, u32[]{:S(2)}) async-start(f32[1,4,512]{2,0,1:T(1,128)} %bitcast.22), calls=%async_computation.2 | async-start | bytes 16384 | tf_op jit(solution)/shard_map/all_to_all | solution.py:153
where the time goes:
time: 381 us; the launch traced here: 379 us
  matrix products  122 us (32%)
  waiting for transfers between devices  102 us (27%)
  other arithmetic  94.4 us (25%)
  local copies, waits for them, and re-layouts  41.2 us (11%)
  starting transfers between devices  18.7 us (5%)
    dot_general x8, matrix products, add_block(): jnp.dot(block, member.astype(jnp.bfloat16), preferred_element_type=jnp.fl...  112 us
    all_to_all x1, waiting for transfers between devices, shards(): lax.all_to_all(planar, 'gz', split_axis=2, concat_axis=1, tiled=True)  90.7 us
    reduce_sum x8, other arithmetic, add_block(): counts = counts + jnp.sum(member.astype(jnp.float32), axis=0)  62.5 us
    convert_element_type x4, other arithmetic, planar_filter(): pieces.append(planar.astype(jnp.bfloat16))  11.2 us
    dynamic_slice x8, local copies, waits for them, and re-layouts, add_block(): lax.dynamic_slice_in_dim(features, start, BZ, 1).reshape(chans, voxels)  8.71 us
  transfers between devices with their start and end apart: 5, of which 4 were waited for; matrix products, arithmetic and copies ran while one was open for 4% of the time, Pallas kernels for 0%

commit v1 on v0

v1 whole, which is shorter than its diff:
```python
import functools

import jax
import jax.numpy as jnp
from jax import lax
from jax.experimental import pallas as pl
from jax.experimental.pallas import tpu as pltpu
from jax.sharding import PartitionSpec as P

TAPS = 5
HALF = TAPS // 2
ITERS = 3
HIGH = lax.Precision.HIGHEST
sharpness = 2.0
LO = 128
ROWS = 4
F32 = jnp.float32
BF16 = jnp.bfloat16


def with_halo(cells, axis, dim, width):
    count = lax.axis_size(axis)
    ends = count - 1
    head = lax.slice_in_dim(cells, 0, width, axis=dim)
    tail = lax.slice_in_dim(cells, cells.shape[dim] - width, cells.shape[dim], axis=dim)
    return jnp.concatenate(
        [
            lax.ppermute(tail, axis, [(i, i + 1) for i in range(ends)]),
            cells,
            lax.ppermute(head, axis, [(i + 1, i) for i in range(ends)]),
        ],
        axis=dim,
    )


def feature_kernel(img, ids, taps, owner, pay_ref, means_ref, shift, across, planar, acc):
    depth, rows, cols = ids.shape
    padded_rows = rows + TAPS - 1
    fragments = means_ref.shape[1]
    highs = fragments // LO
    chans = means_ref.shape[0]
    lanes = pay_ref.shape[0] - chans
    for b in range(TAPS):
        shift[b] = img[:, b : b + cols]
    for e in range(HALF):
        planar[e] = jnp.zeros(planar.shape[1:], F32)
        planar[depth + HALF + e] = jnp.zeros(planar.shape[1:], F32)
    acc[...] = jnp.zeros(acc.shape, F32)

    def tap(kind, at):
        return jnp.broadcast_to(taps[:, kind * TAPS + at : kind * TAPS + at + 1], (chans, cols))

    def plane(z, carry):
        for y in range(padded_rows):
            total = None
            for b in range(TAPS):
                row = shift[b, pl.ds(z * padded_rows + y, 1), :]
                term = tap(0, b) * jnp.broadcast_to(row, (chans, cols))
                total = term if total is None else total + term
            across[y] = total
        for y in range(rows):
            total = tap(1, 0) * across[y]
            for a in range(1, TAPS):
                total = total + tap(1, a) * across[y + a]
            planar[z + HALF, y] = total.astype(BF16).astype(F32)
        return carry

    lax.fori_loop(0, depth, plane, 0)
    low_line = lax.broadcasted_iota(jnp.int32, (LO, cols), 0).astype(F32).astype(BF16)
    high_line = lax.broadcasted_iota(jnp.int32, (16, cols), 0).astype(F32).astype(BF16)
    one = jnp.ones((16, cols), BF16)
    zero = jnp.zeros((16, cols), BF16)

    def gather_sums(step, carry):
        z = step // (rows // ROWS)
        base = (step % (rows // ROWS)) * ROWS
        left, right = [], []
        for r in range(ROWS):
            y = base + r
            total = tap(2, 0) * planar[z, y]
            for e in range(1, TAPS):
                total = total + tap(2, e) * planar[z + e, y]
            feat = jnp.tanh(total).astype(BF16)
            idrow = ids[z, pl.ds(y, 1), :]
            high = jnp.broadcast_to((idrow // LO).astype(F32), (16, cols)).astype(BF16)
            low = jnp.broadcast_to((idrow % LO).astype(F32), (16, cols)).astype(BF16)
            parts = [
                jnp.where(high == jnp.full((16, cols), h, BF16), feat, zero) for h in range(highs)
            ]
            parts.append(jnp.where(high == high_line, one, zero))
            left.append(jnp.concatenate(parts, axis=0))
            right.append(
                jnp.concatenate(
                    [
                        jnp.where(low == low_line[k * 16 : (k + 1) * 16], one, zero)
                        for k in range(LO // 16)
                    ],
                    axis=0,
                )
            )
        acc[...] += lax.dot_general(
            jnp.concatenate(left, axis=1),
            jnp.concatenate(right, axis=1),
            (((1,), (1,)), ((), ())),
            preferred_element_type=F32,
        )
        return carry

    lax.fori_loop(0, depth * (rows // ROWS), gather_sums, 0)
    for h in range(highs):
        count = acc[highs * chans + h : highs * chans + h + 1, :]
        mean = acc[h * chans : (h + 1) * chans, :] / count
        means_ref[:, h * LO : (h + 1) * LO] = mean
        pay_ref[:chans, h * LO : (h + 1) * LO] = mean
        own = jnp.broadcast_to(owner[:, h * LO : (h + 1) * LO], (lanes, LO))
        line = lax.broadcasted_iota(jnp.int32, (lanes, LO), 0)
        pay_ref[chans:, h * LO : (h + 1) * LO] = jnp.where(
            own == line, jnp.broadcast_to(count, (lanes, LO)), 0.0
        )


def split3(x):
    high = x.astype(BF16)
    rest = x - high.astype(F32)
    mid = rest.astype(BF16)
    low = (rest - mid.astype(F32)).astype(BF16)
    return high, mid, low


def refine_kernel(pseudo, pay, weight, coarse, parent, offsets, out_ref, factors, norms):
    sources, chans, fragments = pay.shape
    coarse_count = coarse.shape[1]
    fine = out_ref.shape[1]
    select = (
        jnp.broadcast_to(parent[...], (coarse_count, fine))
        == lax.broadcasted_iota(jnp.int32, (coarse_count, fine), 0)
    ).astype(F32)
    cents = jnp.dot(coarse[...], select, precision=HIGH, preferred_element_type=F32) + offsets[...]

    def prepare(s, carry):
        frags = pay[s]
        fh, fm, fl = split3(-2.0 * frags)
        ones = jnp.ones((3 * chans, fragments), BF16)
        factors[s] = jnp.concatenate([fh, fm, fh, fl, fm, fh, ones], axis=0)
        norms[s] = jnp.sum(frags * frags, axis=0, keepdims=True)
        return carry

    lax.fori_loop(0, sources, prepare, 0)
    for step in range(ITERS):
        ch, cm, cl = split3(cents)
        sh, sm, sl = split3(cents * cents)
        keys = jnp.concatenate([ch, ch, cm, ch, cm, cl, sh, sm, sl], axis=0)

        def visit(s, total):
            distance = norms[s] + lax.dot_general(
                keys, factors[s], (((0,), (0,)), ((), ())), preferred_element_type=F32
            )
            scores = -sharpness * distance
            top = jnp.max(scores, axis=0, keepdims=True)
            expo = jnp.exp(scores - top)
            scale = weight[s] / jnp.sum(expo, axis=0, keepdims=True)
            scale = jnp.broadcast_to(scale, (chans, fragments))
            gh, gm, gl = split3(jnp.concatenate([pay[s] * scale, scale], axis=0))
            eh, em, el = split3(expo)
            dims = (((1,), (1,)), ((), ()))
            first = lax.dot_general(
                jnp.concatenate([gh, gm, gl], axis=0), eh, dims, preferred_element_type=F32
            )
            second = lax.dot_general(
                jnp.concatenate([gh, gm], axis=0), em, dims, preferred_element_type=F32
            )
            size = 2 * chans
            return (
                total
                + (first[2 * size :] + second[size:])
                + (first[size : 2 * size] + second[:size])
                + first[:size]
            )

        total = lax.fori_loop(0, sources, visit, jnp.zeros((2 * chans, fine), F32))
        cents = (total[:chans] + pseudo * cents) / (total[chans:] + pseudo)
    out_ref[...] = cents


def shards(
    slab_image,
    width_taps,
    height_taps,
    depth_taps,
    fragment_ids,
    fragment_owner,
    coarse_centroids,
    parent_map,
    fine_offsets,
):
    chans = width_taps.shape[0]
    depth, rows, cols = fragment_ids.shape
    fragments = fragment_owner.shape[0]
    lanes = lax.axis_size("xy")
    stacks = lax.axis_size("gz")
    padded_rows = rows + TAPS - 1
    rimmed = with_halo(slab_image, "xy", 2, HALF)
    rimmed = jnp.pad(rimmed, ((0, 0), (HALF, HALF), (0, 0)))
    blocks = jnp.stack([rimmed[:, j * rows : j * rows + padded_rows] for j in range(stacks)])
    pencil = lax.all_to_all(blocks, "gz", split_axis=0, concat_axis=0, tiled=True)
    pencil = pencil.reshape(depth * padded_rows, cols + TAPS - 1)
    taps = jnp.concatenate([width_taps, height_taps, depth_taps], axis=1)
    highs = fragments // LO
    assert highs <= 16
    pay, means = pl.pallas_call(
        feature_kernel,
        out_shape=(
            jax.ShapeDtypeStruct((chans + lanes, fragments), F32),
            jax.ShapeDtypeStruct((chans, fragments), F32),
        ),
        in_specs=[pl.BlockSpec(memory_space=pltpu.VMEM)] * 4,
        out_specs=(pl.BlockSpec(memory_space=pltpu.VMEM),) * 2,
        scratch_shapes=[
            pltpu.VMEM((TAPS, depth * padded_rows, cols), F32),
            pltpu.VMEM((padded_rows, chans, cols), F32),
            pltpu.VMEM((depth + 2 * HALF, rows, chans, cols), F32),
            pltpu.VMEM((highs * chans + 16, LO), F32),
        ],
        compiler_params=pltpu.CompilerParams(vmem_limit_bytes=56 << 20),
        name="features",
    )(pencil, fragment_ids, taps, fragment_owner.reshape(1, fragments))
    gathered = lax.all_gather(pay, "xy", axis=0)
    me = lax.axis_index("xy")
    weight = lax.dynamic_slice_in_dim(gathered, chans + me, 1, axis=1)
    fine = fine_offsets.shape[1]
    pseudo = float(fragment_ids.size // fine)
    centroids = pl.pallas_call(
        functools.partial(refine_kernel, pseudo),
        out_shape=jax.ShapeDtypeStruct((chans, fine), F32),
        in_specs=[pl.BlockSpec(memory_space=pltpu.VMEM)] * 5,
        out_specs=pl.BlockSpec(memory_space=pltpu.VMEM),
        scratch_shapes=[
            pltpu.VMEM((lanes, 9 * chans, fragments), BF16),
            pltpu.VMEM((lanes, 1, fragments), F32),
        ],
        compiler_params=pltpu.CompilerParams(vmem_limit_bytes=48 << 20),
        name="refine",
    )(gathered[:, :chans], weight, coarse_centroids, parent_map.reshape(1, fine), fine_offsets)
    return (means, centroids)


def solution(mesh):
    placed = (
        P("gz", None, "xy"),
        P(),
        P(),
        P(),
        P(None, "gz", "xy"),
        P(("gz", "xy"), None),
        P(None, ("gz", "xy")),
        P(("gz", "xy")),
        P(None, ("gz", "xy")),
    )
    return jax.shard_map(
        shards,
        mesh=mesh,
        in_specs=placed,
        out_specs=(P(None, ("gz", "xy")), P(None, ("gz", "xy"))),
        check_vma=False,
    )
```

time: 381 us -> 141 us (0.37)
  matrix products: 122 us -> 0 us
  other arithmetic: 94.4 us -> 1.28 us
  Pallas kernels: 0 us -> 74 us
  waiting for transfers between devices: 102 us -> 36 us
  local copies, waits for them, and re-layouts: 41.2 us -> 8.33 us
  blocking collectives: 0 us -> 9.48 us
  starting transfers between devices: 18.7 us -> 11.2 us
    dot_general x18 -> x0, matrix products: 122 us -> none  [the longest x8 112 us: add_block(): jnp.dot(block, member.astype(jnp.bfloat16), preferred_element_type=jnp.fl...]
    pallas_call x0 -> x2, Pallas kernels: none -> 74 us  [the longest x1 64.6 us: shards(): pl.pallas_call(feature_kernel, out_shape=(jax.ShapeDtypeStruct((chans + l...]
    all_to_all x3 -> x1, waiting for transfers between devices: 94 us -> 24.3 us  [shards(): lax.all_to_all(blocks, 'gz', split_axis=0, concat_axis=0, tiled=True)]
    reduce_sum x13 -> x0, other arithmetic: 63.1 us -> none  [the longest x8 62.5 us: add_block(): counts = counts + jnp.sum(member.astype(jnp.float32), axis=0)]
    dynamic_slice x16 -> x1, local copies, waits for them, and re-layouts: 15.5 us -> 0.02 us  [shards(): weight = lax.dynamic_slice_in_dim(gathered, chans + me, 1, axis=1)]
    convert_element_type x10 -> x0, other arithmetic: 15.5 us -> none  [the longest x4 11.2 us: planar_filter(): pieces.append(planar.astype(jnp.bfloat16))]
    all_gather x0 -> x1, blocking collectives: none -> 9.48 us  [shards(): gathered = lax.all_gather(pay, 'xy', axis=0)]
    all_to_all x3 -> x1, starting transfers between devices: 12.5 us -> 5.01 us  [shards(): lax.all_to_all(blocks, 'gz', split_axis=0, concat_axis=0, tiled=True)]
  transfers between devices with their start and end apart: 5 -> 3, of which waited for: 4 -> 3; matrix products, arithmetic and copies ran while one was open for 4% -> 1% of each run, Pallas kernels for 0% -> 0%
where the time goes in v1:
time: 141 us
  Pallas kernels  74 us (52%)
  waiting for transfers between devices  36 us (26%)
  starting transfers between devices  11.2 us (8%)
  blocking collectives  9.48 us (7%)
  local copies, waits for them, and re-layouts  8.33 us (6%)
    pallas_call x1, Pallas kernels, shards(): pl.pallas_call(feature_kernel, out_shape=(jax.ShapeDtypeStruct((chans + l...  64.6 us
    all_to_all x1, waiting for transfers between devices, shards(): lax.all_to_all(blocks, 'gz', split_axis=0, concat_axis=0, tiled=True)  24.3 us
    all_gather x1, blocking collectives, shards(): gathered = lax.all_gather(pay, 'xy', axis=0)  9.48 us
    pallas_call x1, Pallas kernels, shards(): pl.pallas_call(functools.partial(refine_kernel, pseudo), out_shape=jax.Sh...  9.35 us
    ppermute x1, waiting for transfers between devices, with_halo(): lax.ppermute(head, axis, [(i + 1, i) for i in range(ends)])  7.56 us
    unnamed x23, local copies, waits for them, and re-layouts  6.29 us
    all_to_all x1, starting transfers between devices, shards(): lax.all_to_all(blocks, 'gz', split_axis=0, concat_axis=0, tiled=True)  5.01 us
    ppermute x1, starting transfers between devices, with_halo(): lax.ppermute(tail, axis, [(i, i + 1) for i in range(ends)])  4.86 us
  transfers between devices with their start and end apart: 3, of which 3 were waited for; matrix products, arithmetic and copies ran while one was open for 1% of the time, Pallas kernels for 0%

profile of v1, /device:TPU:0, one launch (start us, length us, event | category | flops | bytes accessed | tf_op | source)
XLA Modules:
  0.0 141.0 jit_solution(14126260540023909439)
XLA Ops:
  0.6 1.4 copy.17
  2.0 0.2 fusion.10
  2.2 4.9 %collective-permute-start = (f32[4,128,2]{2,0,1:T(4,128)S(1)}, f32[4,128,2]{2,0,1:T(4,128)S(1)}, u32[]{:S(2)}, u32[]{:S(2)}) collective-permute-start(f32[4,128,2]{2,0,1:T(4,128)S(1)} %get-tuple-element.6), channel_id=1, source_target_pairs={{0,1},{1,2},{2,3},{4,5},{5,6},{6,7},{8,9},{9,10},{10,11},{12,13},{... | collective-permute-start | bytes 12296 | tf_op jit(solution)/shard_map/ppermute | solution.py:28
  7.1 1.3 collective-permute-start.1
  8.4 4.2 %collective-permute-done = f32[4,128,2]{2,0,1:T(4,128)S(1)} collective-permute-done((f32[4,128,2]{2,0,1:T(4,128)S(1)}, f32[4,128,2]{2,0,1:T(4,128)S(1)}, u32[]{:S(2)}, u32[]{:S(2)}) %collective-permute-start) | collective-permute-done | bytes 4128 | tf_op jit(solution)/shard_map/ppermute | solution.py:28
  12.6 7.6 %collective-permute-done.1 = f32[4,128,2]{2,0,1:T(4,128)S(1)} collective-permute-done((f32[4,128,2]{2,0,1:T(4,128)S(1)}, f32[4,128,2]{2,0,1:T(4,128)S(1)}, u32[]{:S(2)}, u32[]{:S(2)}) %collective-permute-start.1) | collective-permute-done | bytes 4128 | tf_op jit(solution)/shard_map/ppermute | solution.py:30
  20.2 0.6 pad_maximum_fusion
  20.8 0.6 fusion.1
  21.4 0.7 fusion.9
  22.1 0.7 fusion.8
  22.8 0.7 fusion.7
  23.4 0.7 fusion.6
  24.1 0.7 fusion.5
  24.8 0.7 fusion.4
  25.4 0.7 fusion.3
  26.1 0.0 copy-start.3
  26.1 0.0 copy-start.4
  26.1 0.0 copy-start.5
  26.1 5.0 %all-to-all-start = ((f32[8,4,20,260]{3,1,2,0:T(4,128)}), f32[8,4,20,260]{3,1,2,0:T(4,128)S(1)}, u32[]{:S(2)}, u32[]{:S(2)}) async-start(f32[8,4,20,260]{3,1,2,0:T(4,128)} %fusion.3), calls=%async_computation | async-start | bytes 1966080 | tf_op jit(solution)/shard_map/all_to_all | solution.py:205
  31.1 0.0 copy-done.3
  31.1 0.1 copy.21
  31.2 0.0 copy-done.4
  31.2 0.1 copy.22
  31.3 0.0 copy-done.5
  31.3 0.1 copy.23
  31.4 0.7 pad_maximum_fusion.1.taps
  32.0 24.3 %all-to-all-done = f32[8,4,20,260]{3,1,2,0:T(4,128)S(1)} async-done(((f32[8,4,20,260]{3,1,2,0:T(4,128)}), f32[8,4,20,260]{3,1,2,0:T(4,128)S(1)}, u32[]{:S(2)}, u32[]{:S(2)}) %all-to-all-start) | async-done | bytes 665632 | tf_op jit(solution)/shard_map/all_to_all | solution.py:205
  56.3 0.1 copy.20
  56.4 1.0 reshape.13.img
  57.4 0.0 copy-start
  57.4 0.0 copy-start.1
  57.4 0.0 copy-start.2
  57.4 64.6 %features.1 = (f32[20,1024]{1,0:T(8,128)}, f32[16,1024]{1,0:T(8,128)}) custom-call(f32[640,260]{1,0:T(8,128)} %reshape.13.img, s32[32,16,256]{2,1,0:T(8,128)} %ids.1, f32[16,15]{1,0:T(8,128)} %pad_maximum_fusion.1.taps, s32[1,1024]{1,0:T(1,128)} %bitcast.37), custom_call_target="tpu_custom_call" | custom-call | tf_op jit(solution)/shard_map/features/pallas_call | solution.py:210
  122.0 9.5 %all-gather.1 = f32[4,20,1024]{2,1,0:T(8,128)S(1)} all-gather(f32[1,20,1024]{2,1,0:T(8,128)} %bitcast.36), channel_id=2, replica_groups=mesh['gz'=8,'xy'=4] {'xy'}, dimensions={0}, use_global_device_ids=true | all-gather | bytes 409600 | tf_op jit(solution)/shard_map/all_gather | solution.py:227
  131.6 0.0 copy-done
  131.6 0.0 copy-done.1
  131.6 0.0 copy-done.2
  131.6 9.4 %refine.1 = f32[16,128]{1,0:T(8,128)} custom-call(f32[4,16,1024]{2,1,0:T(8,128)S(1)} %slice.58.pay, f32[4,1,1024]{2,1,0:T(1,128)S(1)} %constant_dynamic-slice_fusion.weight, f32[16,32]{1,0:T(8,128)S(1)} %copy-done, s32[1,128]{1,0:T(1,128)S(1)} %bitcast.35, f32[16,128]{1,0:T(8,128)S(1)} %copy-done.1), custom_call_target="tpu_custom_call" | custom-call | tf_op jit(solution)/shard_map/refine/pallas_call | solution.py:232
  (2 shorter events, 0.0 us)
Async XLA Ops:
  2.2 10.4 %collective-permute-start = (f32[4,128,2]{2,0,1:T(4,128)S(1)}, f32[4,128,2]{2,0,1:T(4,128)S(1)}, u32[]{:S(2)}, u32[]{:S(2)}) collective-permute-start(f32[4,128,2]{2,0,1:T(4,128)S(1)} %get-tuple-element.6), channel_id=1, source_target_pairs={{0,1},{1,2},{2,3},{4,5},{5,6},{6,7},{8,9},{9,10},{10,11},{12,13},{... | collective-permute-start | bytes 12296 | tf_op jit(solution)/shard_map/ppermute | solution.py:28
  7.1 13.1 %collective-permute-start.1 = (f32[4,128,2]{2,0,1:T(4,128)S(1)}, f32[4,128,2]{2,0,1:T(4,128)S(1)}, u32[]{:S(2)}, u32[]{:S(2)}) collective-permute-start(f32[4,128,2]{2,0,1:T(4,128)S(1)} %get-tuple-element.7), channel_id=1, source_target_pairs={{1,0},{2,1},{3,2},{5,4},{6,5},{7,6},{9,8},{10,9},{11,10},{13,12},{... | collective-permute-start | bytes 12296 | tf_op jit(solution)/shard_map/ppermute | solution.py:30
  26.1 5.0 %copy-start.3 = (f32[16,5]{0,1:T(8,128)S(1)}, f32[16,5]{0,1:T(8,128)}, u32[]{:S(2)}) copy-start(f32[16,5]{0,1:T(8,128)} %param.10) | copy-start | bytes 964
  26.1 5.1 %copy-start.4 = (f32[16,5]{0,1:T(8,128)S(1)}, f32[16,5]{0,1:T(8,128)}, u32[]{:S(2)}) copy-start(f32[16,5]{0,1:T(8,128)} %param.11) | copy-start | bytes 964
  26.1 5.2 %copy-start.5 = (f32[16,5]{0,1:T(8,128)S(1)}, f32[16,5]{0,1:T(8,128)}, u32[]{:S(2)}) copy-start(f32[16,5]{0,1:T(8,128)} %param.12) | copy-start | bytes 964
  26.1 30.2 %all-to-all-start = ((f32[8,4,20,260]{3,1,2,0:T(4,128)}), f32[8,4,20,260]{3,1,2,0:T(4,128)S(1)}, u32[]{:S(2)}, u32[]{:S(2)}) async-start(f32[8,4,20,260]{3,1,2,0:T(4,128)} %fusion.3), calls=%async_computation | async-start | bytes 1966080 | tf_op jit(solution)/shard_map/all_to_all | solution.py:205
  57.4 74.1 %copy-start = (f32[16,32]{1,0:T(8,128)S(1)}, f32[16,32]{1,0:T(8,128)}, u32[]{:S(2)}) copy-start(f32[16,32]{1,0:T(8,128)} %coarse.1) | copy-start | bytes 6148
  57.4 74.2 %copy-start.1 = (f32[16,128]{1,0:T(8,128)S(1)}, f32[16,128]{1,0:T(8,128)}, u32[]{:S(2)}) copy-start(f32[16,128]{1,0:T(8,128)} %offsets.1) | copy-start | bytes 24580
  57.4 74.2 %copy-start.2 = (s32[128]{0:T(128)S(1)}, s32[128]{0:T(128)}, u32[]{:S(2)}) copy-start(s32[128]{0:T(128)} %param.16) | copy-start | bytes 1540

commit v2 on v1

v2 whole, which is shorter than its diff:
```python
import functools

import jax
import jax.numpy as jnp
from jax import lax
from jax.experimental import pallas as pl
from jax.experimental.pallas import tpu as pltpu
from jax.sharding import PartitionSpec as P

TAPS = 5
HALF = TAPS // 2
ITERS = 3
HIGH = lax.Precision.HIGHEST
sharpness = 2.0
LO = 128
ROWS = 4
F32 = jnp.float32
BF16 = jnp.bfloat16


MESH = pl.DeviceIdType.MESH
LANE = 128


def exchange_kernel(rows, img, out, blocks, edges, halo, turned, send, recv, side_send, side_recv):
    here = lax.axis_index("gz")
    lane = lax.axis_index("xy")
    stacks = lax.axis_size("gz")
    lanes = lax.axis_size("xy")
    depth, height, cols = img.shape
    padded = rows + TAPS - 1
    size = depth * padded
    wide = depth * HALF

    for side in range(2):
        if stacks * wide < LANE:
            halo[side, stacks * wide :, :] = jnp.zeros((LANE - stacks * wide, height), F32)

    @pl.when(lane == 0)
    def _():
        halo[0] = jnp.zeros(halo.shape[1:], F32)

    @pl.when(lane == lanes - 1)
    def _():
        halo[1] = jnp.zeros(halo.shape[1:], F32)

    barrier = pltpu.get_barrier_semaphore()

    def greet(d, carry):
        j = lax.rem(here + d, stacks)

        @pl.when(d > 0)
        def _():
            pl.semaphore_signal(barrier, inc=1, device_id=(j, lane), device_id_type=MESH)

        @pl.when(lane > 0)
        def _():
            pl.semaphore_signal(barrier, inc=1, device_id=(j, lane - 1), device_id_type=MESH)

        @pl.when(lane < lanes - 1)
        def _():
            pl.semaphore_signal(barrier, inc=1, device_id=(j, lane + 1), device_id_type=MESH)

        return carry

    lax.fori_loop(0, stacks, greet, 0)
    for j in range(stacks):
        for z in range(depth):
            start = j * rows - HALF
            low, high = max(start, 0), min(start + padded, height)
            at = z * padded
            if low > start:
                blocks[j, at : at + low - start, :] = jnp.zeros((low - start, cols), F32)
            if high < start + padded:
                blocks[j, at + high - start : at + padded, :] = jnp.zeros(
                    (start + padded - high, cols), F32
                )
            blocks[j, at + low - start : at + high - start, :] = img[z, low:high, :]
    for z in range(depth):
        first = jnp.transpose(img[z, :, :LANE])
        last = jnp.transpose(img[z, :, cols - LANE :])
        edges[0, z * HALF : (z + 1) * HALF, :] = last[LANE - HALF :, :]
        edges[1, z * HALF : (z + 1) * HALF, :] = first[:HALF, :]
    sides = lax.div(lane + lanes - 1, lanes) + lax.div(2 * lanes - 2 - lane, lanes)
    pl.semaphore_wait(barrier, stacks - 1 + stacks * sides)

    def main_copy(j, source):
        return pltpu.make_async_remote_copy(
            src_ref=blocks.at[j],
            dst_ref=out.at[pl.ds(pl.multiple_of(source * size, 8), size), LANE : LANE + cols],
            send_sem=send.at[j],
            recv_sem=recv.at[source],
            device_id=(j, lane),
            device_id_type=MESH,
        )

    def side_copy(side, j, source, target):
        return pltpu.make_async_remote_copy(
            src_ref=edges.at[side],
            dst_ref=halo.at[side, pl.ds(pl.multiple_of(source * wide, 8), wide), :],
            send_sem=side_send.at[side, j],
            recv_sem=side_recv.at[side, source],
            device_id=(j, target),
            device_id_type=MESH,
        )

    def start(d, carry):
        j = lax.rem(here + d, stacks)

        @pl.when(d > 0)
        def _():
            main_copy(j, here).start()

        @pl.when(lane < lanes - 1)
        def _():
            side_copy(0, j, here, lane + 1).start()

        @pl.when(lane > 0)
        def _():
            side_copy(1, j, here, lane - 1).start()

        return carry

    lax.fori_loop(0, stacks, start, 0)
    out[pl.ds(pl.multiple_of(here * size, 8), size), LANE : LANE + cols] = blocks[here]

    def finish(d, carry):
        j = lax.rem(here + d, stacks)

        @pl.when(d > 0)
        def _():
            main_copy(j, here).wait_send()
            main_copy(j, j).wait_recv()

        @pl.when(lane < lanes - 1)
        def _():
            side_copy(0, j, here, lane + 1).wait_send()
            side_copy(1, j, j, lane + 1).wait_recv()

        @pl.when(lane > 0)
        def _():
            side_copy(1, j, here, lane - 1).wait_send()
            side_copy(0, j, j, lane - 1).wait_recv()

        return carry

    lax.fori_loop(0, stacks, finish, 0)
    for side in range(2):
        turned[:8, :] = jnp.zeros((8, LANE), F32)
        turned[8 + height :, :] = jnp.zeros((8, LANE), F32)
        turned[8 : 8 + height, :] = jnp.transpose(halo[side])
        strip = turned[pl.ds(here * rows + 8 - HALF, padded), :]
        for z in range(stacks * depth):
            place = LANE - HALF if side == 0 else LANE + cols
            out[z * padded : (z + 1) * padded, place : place + HALF] = strip[
                :, z * HALF : (z + 1) * HALF
            ]


def gather_kernel(pay, out, send, recv):
    here = lax.axis_index("gz")
    lane = lax.axis_index("xy")
    lanes = lax.axis_size("xy")
    barrier = pltpu.get_barrier_semaphore()
    for d in range(1, lanes):
        pl.semaphore_signal(
            barrier, inc=1, device_id=(here, lax.rem(lane + d, lanes)), device_id_type=MESH
        )
    pl.semaphore_wait(barrier, lanes - 1)

    def copy(target, source):
        return pltpu.make_async_remote_copy(
            src_ref=pay,
            dst_ref=out.at[source],
            send_sem=send.at[target],
            recv_sem=recv.at[source],
            device_id=(here, target),
            device_id_type=MESH,
        )

    for d in range(1, lanes):
        copy(lax.rem(lane + d, lanes), lane).start()
    out[lane] = pay[...]
    for d in range(1, lanes):
        other = lax.rem(lane + d, lanes)
        copy(other, lane).wait_send()
        copy(other, other).wait_recv()


def feature_kernel(img, ids, taps, owner, pay_ref, means_ref, shift, planar, highs_f, lows_f, acc):
    depth, rows, cols = ids.shape
    padded_rows = rows + TAPS - 1
    fragments = means_ref.shape[1]
    highs = fragments // LO
    chans = means_ref.shape[0]
    lanes = pay_ref.shape[0] - chans
    for b in range(TAPS):
        for x in range(0, cols, LANE):
            start = LANE - HALF + b + x
            shift[b, x // LANE] = img[:, start : start + LANE]
    for e in range(HALF):
        planar[e] = jnp.zeros(planar.shape[1:], F32)
        planar[depth + HALF + e] = jnp.zeros(planar.shape[1:], F32)
    acc[...] = jnp.zeros(acc.shape, F32)

    def divide(z, carry):
        for x in range(0, cols, LANE):
            part = ids[z, :, x : x + LANE]
            highs_f[x // LANE, z] = (part >> (LO.bit_length() - 1)).astype(F32)
            lows_f[x // LANE, z] = (part & (LO - 1)).astype(F32)
        return carry

    lax.fori_loop(0, depth, divide, 0)
    tap = [jnp.broadcast_to(taps[:, i : i + 1], (chans, LANE)) for i in range(3 * TAPS)]

    def plane(z, carry):
        for x in range(0, cols, LANE):
            window = []
            for y in range(padded_rows):
                total = None
                for b in range(TAPS):
                    row = shift[b, x // LANE, pl.ds(z * padded_rows + y, 1), :]
                    term = tap[b] * jnp.broadcast_to(row, (chans, LANE))
                    total = term if total is None else total + term
                window.append(total)
                if y >= TAPS - 1:
                    total = tap[TAPS] * window[y - TAPS + 1]
                    for a in range(1, TAPS):
                        total = total + tap[TAPS + a] * window[y - TAPS + 1 + a]
                    planar[z + HALF, y - TAPS + 1, :, x : x + LANE] = total.astype(BF16).astype(F32)
        return carry

    lax.fori_loop(0, depth, plane, 0)
    low_line = lax.broadcasted_iota(jnp.int32, (LO, LANE), 0).astype(F32).astype(BF16)
    one = jnp.ones((16, LANE), BF16)
    zero = jnp.zeros((16, LANE), BF16)

    def gather_sums(step, carry):
        z = step // (rows // ROWS)
        base = (step % (rows // ROWS)) * ROWS
        left, right = [], []
        for r in range(ROWS):
            y = base + r
            for x in range(0, cols, LANE):
                total = tap[2 * TAPS] * planar[z, y, :, x : x + LANE]
                for e in range(1, TAPS):
                    total = total + tap[2 * TAPS + e] * planar[z + e, y, :, x : x + LANE]
                feat = jnp.tanh(total).astype(BF16)
                high = highs_f[x // LANE, z, pl.ds(y, 1), :]
                high = jnp.broadcast_to(high, (16, LANE)).astype(BF16)
                low = lows_f[x // LANE, z, pl.ds(y, 1), :]
                low = jnp.broadcast_to(low, (16, LANE)).astype(BF16)
                parts = [
                    jnp.where(high == jnp.full((16, LANE), h, BF16), feat, zero)
                    for h in range(highs)
                ]
                parts.append(jnp.where(high == low_line[:16], one, zero))
                left.append(jnp.concatenate(parts, axis=0))
                right.append(
                    jnp.concatenate(
                        [
                            jnp.where(low == low_line[k * 16 : (k + 1) * 16], one, zero)
                            for k in range(LO // 16)
                        ],
                        axis=0,
                    )
                )
        acc[...] += lax.dot_general(
            jnp.concatenate(left, axis=1),
            jnp.concatenate(right, axis=1),
            (((1,), (1,)), ((), ())),
            preferred_element_type=F32,
        )
        return carry

    lax.fori_loop(0, depth * (rows // ROWS), gather_sums, 0)
    for h in range(highs):
        count = acc[highs * chans + h : highs * chans + h + 1, :]
        mean = acc[h * chans : (h + 1) * chans, :] / count
        means_ref[:, h * LO : (h + 1) * LO] = mean
        pay_ref[:chans, h * LO : (h + 1) * LO] = mean
        own = jnp.broadcast_to(owner[:, h * LO : (h + 1) * LO], (lanes, LO))
        line = lax.broadcasted_iota(jnp.int32, (lanes, LO), 0)
        pay_ref[chans:, h * LO : (h + 1) * LO] = jnp.where(
            own == line, jnp.broadcast_to(count, (lanes, LO)), 0.0
        )


def split3(x):
    high = x.astype(BF16)
    rest = x - high.astype(F32)
    mid = rest.astype(BF16)
    low = (rest - mid.astype(F32)).astype(BF16)
    return high, mid, low


def refine_kernel(pseudo, pay, coarse, parent, offsets, out_ref, factors, norms):
    sources, _, fragments = pay.shape
    chans = out_ref.shape[0]
    own = chans + lax.axis_index("xy")
    coarse_count = coarse.shape[1]
    fine = out_ref.shape[1]
    select = (
        jnp.broadcast_to(parent[...], (coarse_count, fine))
        == lax.broadcasted_iota(jnp.int32, (coarse_count, fine), 0)
    ).astype(F32)
    cents = jnp.dot(coarse[...], select, precision=HIGH, preferred_element_type=F32) + offsets[...]

    def prepare(s, carry):
        frags = pay[s, :chans, :]
        fh, fm, fl = split3(-2.0 * frags)
        ones = jnp.ones((3 * chans, fragments), BF16)
        factors[s] = jnp.concatenate([fh, fm, fh, fl, fm, fh, ones], axis=0)
        norms[s] = jnp.sum(frags * frags, axis=0, keepdims=True)
        return carry

    lax.fori_loop(0, sources, prepare, 0)
    for step in range(ITERS):
        ch, cm, cl = split3(cents)
        sh, sm, sl = split3(cents * cents)
        keys = jnp.concatenate([ch, ch, cm, ch, cm, cl, sh, sm, sl], axis=0)

        def visit(s, total):
            distance = norms[s] + lax.dot_general(
                keys, factors[s], (((0,), (0,)), ((), ())), preferred_element_type=F32
            )
            scores = -sharpness * distance
            top = jnp.max(scores, axis=0, keepdims=True)
            expo = jnp.exp(scores - top)
            scale = pay[s, pl.ds(own, 1), :] / jnp.sum(expo, axis=0, keepdims=True)
            scale = jnp.broadcast_to(scale, (chans, fragments))
            gh, gm, gl = split3(jnp.concatenate([pay[s, :chans, :] * scale, scale], axis=0))
            eh, em, el = split3(expo)
            dims = (((1,), (1,)), ((), ()))
            first = lax.dot_general(
                jnp.concatenate([gh, gm, gl], axis=0), eh, dims, preferred_element_type=F32
            )
            second = lax.dot_general(
                jnp.concatenate([gh, gm], axis=0), em, dims, preferred_element_type=F32
            )
            size = 2 * chans
            return (
                total
                + (first[2 * size :] + second[size:])
                + (first[size : 2 * size] + second[:size])
                + first[:size]
            )

        total = lax.fori_loop(0, sources, visit, jnp.zeros((2 * chans, fine), F32))
        cents = (total[:chans] + pseudo * cents) / (total[chans:] + pseudo)
    out_ref[...] = cents


def shards(
    slab_image,
    width_taps,
    height_taps,
    depth_taps,
    fragment_ids,
    fragment_owner,
    coarse_centroids,
    parent_map,
    fine_offsets,
):
    chans = width_taps.shape[0]
    depth, rows, cols = fragment_ids.shape
    fragments = fragment_owner.shape[0]
    lanes = lax.axis_size("xy")
    stacks = lax.axis_size("gz")
    padded_rows = rows + TAPS - 1
    slab_depth, height, _ = slab_image.shape
    pencil = pl.pallas_call(
        functools.partial(exchange_kernel, rows),
        out_shape=jax.ShapeDtypeStruct((depth * padded_rows, cols + 2 * LANE), F32),
        in_specs=[pl.BlockSpec(memory_space=pltpu.VMEM)],
        out_specs=pl.BlockSpec(memory_space=pltpu.VMEM),
        scratch_shapes=[
            pltpu.VMEM((stacks, slab_depth * padded_rows, cols), F32),
            pltpu.VMEM((2, slab_depth * HALF, height), F32),
            pltpu.VMEM((2, LANE, height), F32),
            pltpu.VMEM((height + 16, LANE), F32),
            pltpu.SemaphoreType.DMA((stacks,)),
            pltpu.SemaphoreType.DMA((stacks,)),
            pltpu.SemaphoreType.DMA((2, stacks)),
            pltpu.SemaphoreType.DMA((2, stacks)),
        ],
        compiler_params=pltpu.CompilerParams(
            collective_id=0, has_side_effects=True, vmem_limit_bytes=32 << 20
        ),
        name="exchange",
    )(slab_image)
    taps = jnp.concatenate([width_taps, height_taps, depth_taps], axis=1)
    highs = fragments // LO
    assert highs <= 16
    pay, means = pl.pallas_call(
        feature_kernel,
        out_shape=(
            jax.ShapeDtypeStruct((chans + lanes, fragments), F32),
            jax.ShapeDtypeStruct((chans, fragments), F32),
        ),
        in_specs=[pl.BlockSpec(memory_space=pltpu.VMEM)] * 4,
        out_specs=(pl.BlockSpec(memory_space=pltpu.VMEM),) * 2,
        scratch_shapes=[
            pltpu.VMEM((TAPS, cols // LANE, depth * padded_rows, LANE), F32),
            pltpu.VMEM((depth + 2 * HALF, rows, chans, cols), F32),
            pltpu.VMEM((cols // LANE, depth, rows, LANE), F32),
            pltpu.VMEM((cols // LANE, depth, rows, LANE), F32),
            pltpu.VMEM((highs * chans + 16, LO), F32),
        ],
        compiler_params=pltpu.CompilerParams(vmem_limit_bytes=56 << 20),
        name="features",
    )(pencil, fragment_ids, taps, fragment_owner.reshape(1, fragments))
    gathered = pl.pallas_call(
        gather_kernel,
        out_shape=jax.ShapeDtypeStruct((lanes,) + pay.shape, F32),
        in_specs=[pl.BlockSpec(memory_space=pltpu.VMEM)],
        out_specs=pl.BlockSpec(memory_space=pltpu.VMEM),
        scratch_shapes=[pltpu.SemaphoreType.DMA((lanes,)), pltpu.SemaphoreType.DMA((lanes,))],
        compiler_params=pltpu.CompilerParams(
            collective_id=1, has_side_effects=True, vmem_limit_bytes=32 << 20
        ),
        name="gather",
    )(pay)
    fine = fine_offsets.shape[1]
    pseudo = float(fragment_ids.size // fine)
    centroids = pl.pallas_call(
        functools.partial(refine_kernel, pseudo),
        out_shape=jax.ShapeDtypeStruct((chans, fine), F32),
        in_specs=[pl.BlockSpec(memory_space=pltpu.VMEM)] * 4,
        out_specs=pl.BlockSpec(memory_space=pltpu.VMEM),
        scratch_shapes=[
            pltpu.VMEM((lanes, 9 * chans, fragments), BF16),
            pltpu.VMEM((lanes, 1, fragments), F32),
        ],
        compiler_params=pltpu.CompilerParams(vmem_limit_bytes=48 << 20),
        name="refine",
    )(gathered, coarse_centroids, parent_map.reshape(1, fine), fine_offsets)
    return (means, centroids)


def solution(mesh):
    placed = (
        P("gz", None, "xy"),
        P(),
        P(),
        P(),
        P(None, "gz", "xy"),
        P(("gz", "xy"), None),
        P(None, ("gz", "xy")),
        P(("gz", "xy")),
        P(None, ("gz", "xy")),
    )
    return jax.shard_map(
        shards,
        mesh=mesh,
        in_specs=placed,
        out_specs=(P(None, ("gz", "xy")), P(None, ("gz", "xy"))),
        check_vma=False,
    )
```

time: 141 us -> 88.2 us (0.63)
  the two profiles are of different devices: /device:TPU:0 before, /device:TPU:25 now
where the time goes in v2:
time: 88.2 us; the launch traced here: 87.9 us
  Pallas kernels  81.2 us (92%)
  local copies, waits for them, and re-layouts  5.31 us (6%)
    pallas_call x1, Pallas kernels, shards(): pl.pallas_call(feature_kernel, out_shape=(jax.ShapeDtypeStruct((chans + l...  42 us
    pallas_call x1, Pallas kernels, shards(): pl.pallas_call(functools.partial(exchange_kernel, rows), out_shape=jax.Sh...  22.2 us
    pallas_call x1, Pallas kernels, shards(): pl.pallas_call(functools.partial(refine_kernel, pseudo), out_shape=jax.Sh...  9.35 us
    pallas_call x1, Pallas kernels, shards(): pl.pallas_call(gather_kernel, out_shape=jax.ShapeDtypeStruct((lanes,) + p...  7.62 us
    unnamed x15, local copies, waits for them, and re-layouts  5.31 us

profile of v2, /device:TPU:25, one launch (start us, length us, event | category | flops | bytes accessed | tf_op | source)
XLA Modules:
  0.0 87.9 jit_solution(376120983035848027)
XLA Ops:
  0.6 0.8 copy.11
  1.4 0.8 copy.12
  2.2 0.8 copy.13
  2.9 0.7 pad_maximum_fusion.taps
  3.6 0.0 copy-start.1
  3.6 1.0 %copy-done.1 = f32[4,128,256]{2,1,0:T(8,128)S(1)} copy-done((f32[4,128,256]{2,1,0:T(8,128)S(1)}, f32[4,128,256]{2,1,0:T(8,128)}, u32[]{:S(2)}) %copy-start.1) | copy-done | bytes 524312
  4.6 22.2 %exchange.1.img = f32[640,512]{1,0:T(8,128)S(1)} custom-call(f32[4,128,256]{2,1,0:T(8,128)S(1)} %copy-done.1), custom_call_target="tpu_custom_call" | custom-call | tf_op jit(solution)/shard_map/exchange/pallas_call | solution.py:372
  26.8 0.0 copy-start
  26.9 1.1 %copy-done = f32[640,512]{1,0:T(8,128)} copy-done((f32[640,512]{1,0:T(8,128)}, f32[640,512]{1,0:T(8,128)S(1)}, u32[]{:S(2)}) %copy-start) | copy-done | bytes 1310744
  27.9 0.0 copy-start.3
  27.9 0.0 copy-start.4
  27.9 0.0 copy-start.5
  27.9 42.0 %features.1 = (f32[20,1024]{1,0:T(8,128)}, f32[16,1024]{1,0:T(8,128)}) custom-call(f32[640,512]{1,0:T(8,128)} %copy-done, s32[32,16,256]{2,1,0:T(8,128)} %ids.1, f32[16,15]{1,0:T(8,128)} %pad_maximum_fusion.taps, s32[1,1024]{1,0:T(1,128)} %bitcast.3), custom_call_target="tpu_custom_call" | custom-call | tf_op jit(solution)/shard_map/features/pallas_call | solution.py:395
  70.0 0.0 copy-start.2
  70.0 0.9 %copy-done.2 = f32[20,1024]{1,0:T(8,128)S(1)} copy-done((f32[20,1024]{1,0:T(8,128)S(1)}, f32[20,1024]{1,0:T(8,128)}, u32[]{:S(2)}) %copy-start.2) | copy-done | bytes 81944
  70.9 7.6 %gather.1.pay = f32[4,20,1024]{2,1,0:T(8,128)S(1)} custom-call(f32[20,1024]{1,0:T(8,128)S(1)} %copy-done.2), custom_call_target="tpu_custom_call" | custom-call | tf_op jit(solution)/shard_map/gather/pallas_call | solution.py:413
  78.5 0.0 copy-done.3
  78.5 0.0 copy-done.4
  78.5 0.0 copy-done.5
  78.5 9.3 %refine.1 = f32[16,128]{1,0:T(8,128)} custom-call(f32[4,20,1024]{2,1,0:T(8,128)S(1)} %gather.1.pay, f32[16,32]{1,0:T(8,128)S(1)} %copy-done.3, s32[1,128]{1,0:T(1,128)S(1)} %bitcast.2, f32[16,128]{1,0:T(8,128)S(1)} %copy-done.4), custom_call_target="tpu_custom_call" | custom-call | tf_op jit(solution)/shard_map/refine/pallas_call | solution.py:426
Async XLA Ops:
  3.6 1.0 %copy-start.1 = (f32[4,128,256]{2,1,0:T(8,128)S(1)}, f32[4,128,256]{2,1,0:T(8,128)}, u32[]{:S(2)}) copy-start(f32[4,128,256]{2,1,0:T(8,128)} %img.1) | copy-start | bytes 1572868
  26.8 1.1 %copy-start = (f32[640,512]{1,0:T(8,128)}, f32[640,512]{1,0:T(8,128)S(1)}, u32[]{:S(2)}) copy-start(f32[640,512]{1,0:T(8,128)S(1)} %exchange.1.img) | copy-start | bytes 3932164
  27.9 50.6 %copy-start.3 = (f32[16,32]{1,0:T(8,128)S(1)}, f32[16,32]{1,0:T(8,128)}, u32[]{:S(2)}) copy-start(f32[16,32]{1,0:T(8,128)} %coarse.1) | copy-start | bytes 6148
  27.9 50.6 %copy-start.4 = (f32[16,128]{1,0:T(8,128)S(1)}, f32[16,128]{1,0:T(8,128)}, u32[]{:S(2)}) copy-start(f32[16,128]{1,0:T(8,128)} %offsets.1) | copy-start | bytes 24580
  27.9 50.6 %copy-start.5 = (s32[128]{0:T(128)S(1)}, s32[128]{0:T(128)}, u32[]{:S(2)}) copy-start(s32[128]{0:T(128)} %param.16) | copy-start | bytes 1540
  70.0 0.9 %copy-start.2 = (f32[20,1024]{1,0:T(8,128)S(1)}, f32[20,1024]{1,0:T(8,128)}, u32[]{:S(2)}) copy-start(f32[20,1024]{1,0:T(8,128)} %get-tuple-element.5.pay) | copy-start | bytes 245764

commit v3 on v2

--- a/solution.py
+++ b/solution.py
@@ -13,7 +13,7 @@
 HIGH = lax.Precision.HIGHEST
 sharpness = 2.0
 LO = 128
-ROWS = 4
+ROWS = 16
 F32 = jnp.float32
 BF16 = jnp.bfloat16
 
@@ -105,9 +105,9 @@
         )
 
     def start(d, carry):
-        j = lax.rem(here + d, stacks)
-
-        @pl.when(d > 0)
+        j = lax.rem(here + lax.rem(d + stacks // 2, stacks), stacks)
+
+        @pl.when(j != here)
         def _():
             main_copy(j, here).start()
 
@@ -187,7 +187,10 @@
         copy(other, other).wait_recv()
 
 
-def feature_kernel(img, ids, taps, owner, pay_ref, means_ref, shift, planar, highs_f, lows_f, acc):
+def feature_kernel(
+    img, ids, wide, tall, deep, owner, pay_ref, means_ref,
+    shift, planar, highs_f, lows_f, acc, square, *pairs,
+):
     depth, rows, cols = ids.shape
     padded_rows = rows + TAPS - 1
     fragments = means_ref.shape[1]
@@ -211,7 +214,15 @@
         return carry
 
     lax.fori_loop(0, depth, divide, 0)
-    tap = [jnp.broadcast_to(taps[:, i : i + 1], (chans, LANE)) for i in range(3 * TAPS)]
+    square[...] = jnp.zeros(square.shape, F32)
+    for kind, part in enumerate((wide, tall, deep)):
+        square[kind * 8 : kind * 8 + TAPS, :chans] = part[...]
+    turned = jnp.transpose(square[...])
+    tap = [
+        jnp.broadcast_to(turned[:chans, k * 8 + i : k * 8 + i + 1], (chans, LANE))
+        for k in range(3)
+        for i in range(TAPS)
+    ]
 
     def plane(z, carry):
         for x in range(0, cols, LANE):
@@ -235,13 +246,16 @@
     one = jnp.ones((16, LANE), BF16)
     zero = jnp.zeros((16, LANE), BF16)
 
-    def gather_sums(step, carry):
-        z = step // (rows // ROWS)
-        base = (step % (rows // ROWS)) * ROWS
-        left, right = [], []
+    per_plane = rows // ROWS
+    steps = depth * per_plane
+
+    def build(step, left, right):
+        z = step // per_plane
+        base = (step % per_plane) * ROWS
         for r in range(ROWS):
             y = base + r
             for x in range(0, cols, LANE):
+                at = r * cols + x
                 total = tap[2 * TAPS] * planar[z, y, :, x : x + LANE]
                 for e in range(1, TAPS):
                     total = total + tap[2 * TAPS + e] * planar[z + e, y, :, x : x + LANE]
@@ -250,30 +264,32 @@
                 high = jnp.broadcast_to(high, (16, LANE)).astype(BF16)
                 low = lows_f[x // LANE, z, pl.ds(y, 1), :]
                 low = jnp.broadcast_to(low, (16, LANE)).astype(BF16)
-                parts = [
-                    jnp.where(high == jnp.full((16, LANE), h, BF16), feat, zero)
-                    for h in range(highs)
-                ]
-                parts.append(jnp.where(high == low_line[:16], one, zero))
-                left.append(jnp.concatenate(parts, axis=0))
-                right.append(
-                    jnp.concatenate(
-                        [
-                            jnp.where(low == low_line[k * 16 : (k + 1) * 16], one, zero)
-                            for k in range(LO // 16)
-                        ],
-                        axis=0,
+                for h in range(highs):
+                    left[h * 16 : (h + 1) * 16, at : at + LANE] = jnp.where(
+                        high == jnp.full((16, LANE), h, BF16), feat, zero
                     )
-                )
+                left[highs * 16 :, at : at + LANE] = jnp.where(high == low_line[:16], one, zero)
+                for k in range(LO // 16):
+                    right[k * 16 : (k + 1) * 16, at : at + LANE] = jnp.where(
+                        low == low_line[k * 16 : (k + 1) * 16], one, zero
+                    )
+
+    def fire(left, right):
         acc[...] += lax.dot_general(
-            jnp.concatenate(left, axis=1),
-            jnp.concatenate(right, axis=1),
-            (((1,), (1,)), ((), ())),
-            preferred_element_type=F32,
-        )
-        return carry
-
-    lax.fori_loop(0, depth * (rows // ROWS), gather_sums, 0)
+            left[...], right[...], (((1,), (1,)), ((), ())), preferred_element_type=F32
+        )
+
+    left_a, right_a, left_b, right_b = pairs
+    build(0, left_a, right_a)
+
+    def two_steps(pair, carry):
+        fire(left_a, right_a)
+        build(2 * pair + 1, left_b, right_b)
+        fire(left_b, right_b)
+        build(jnp.minimum(2 * pair + 2, steps - 1), left_a, right_a)
+        return carry
+
+    lax.fori_loop(0, steps // 2, two_steps, 0)
     for h in range(highs):
         count = acc[highs * chans + h : highs * chans + h + 1, :]
         mean = acc[h * chans : (h + 1) * chans, :] / count
@@ -314,7 +330,7 @@
         norms[s] = jnp.sum(frags * frags, axis=0, keepdims=True)
         return carry
 
-    lax.fori_loop(0, sources, prepare, 0)
+    lax.fori_loop(0, sources, prepare, 0, unroll=4)
     for step in range(ITERS):
         ch, cm, cl = split3(cents)
         sh, sm, sl = split3(cents * cents)
@@ -346,7 +362,9 @@
                 + first[:size]
             )
 
-        total = lax.fori_loop(0, sources, visit, jnp.zeros((2 * chans, fine), F32))
+        total = lax.fori_loop(
+            0, sources, visit, jnp.zeros((2 * chans, fine), F32), unroll=4
+        )
         cents = (total[:chans] + pseudo * cents) / (total[chans:] + pseudo)
     out_ref[...] = cents
 
@@ -389,7 +407,6 @@
         ),
         name="exchange",
     )(slab_image)
-    taps = jnp.concatenate([width_taps, height_taps, depth_taps], axis=1)
     highs = fragments // LO
     assert highs <= 16
     pay, means = pl.pallas_call(
@@ -398,7 +415,7 @@
             jax.ShapeDtypeStruct((chans + lanes, fragments), F32),
             jax.ShapeDtypeStruct((chans, fragments), F32),
         ),
-        in_specs=[pl.BlockSpec(memory_space=pltpu.VMEM)] * 4,
+        in_specs=[pl.BlockSpec(memory_space=pltpu.VMEM)] * 6,
         out_specs=(pl.BlockSpec(memory_space=pltpu.VMEM),) * 2,
         scratch_shapes=[
             pltpu.VMEM((TAPS, cols // LANE, depth * padded_rows, LANE), F32),
@@ -406,10 +423,15 @@
             pltpu.VMEM((cols // LANE, depth, rows, LANE), F32),
             pltpu.VMEM((cols // LANE, depth, rows, LANE), F32),
             pltpu.VMEM((highs * chans + 16, LO), F32),
+            pltpu.VMEM((LANE, LANE), F32),
+            pltpu.VMEM((highs * chans + 16, ROWS * cols), BF16),
+            pltpu.VMEM((LO, ROWS * cols), BF16),
+            pltpu.VMEM((highs * chans + 16, ROWS * cols), BF16),
+            pltpu.VMEM((LO, ROWS * cols), BF16),
         ],
         compiler_params=pltpu.CompilerParams(vmem_limit_bytes=56 << 20),
         name="features",
-    )(pencil, fragment_ids, taps, fragment_owner.reshape(1, fragments))
+    )(pencil, fragment_ids, width_taps.T, height_taps.T, depth_taps.T, fragment_owner.reshape(1, fragments))
     gathered = pl.pallas_call(
         gather_kernel,
         out_shape=jax.ShapeDtypeStruct((lanes,) + pay.shape, F32),

time: 88.2 us -> 76.5 us (0.87)
  the two profiles are of different devices: /device:TPU:25 before, /device:TPU:0 now
where the time goes in v3:
time: 76.5 us; the launch traced here: 76.2 us
  Pallas kernels  72.5 us (95%)
  local copies, waits for them, and re-layouts  3.01 us (4%)
    pallas_call x1, Pallas kernels, shards(): pl.pallas_call(feature_kernel, out_shape=(jax.ShapeDtypeStruct((chans + l...  34 us
    pallas_call x1, Pallas kernels, shards(): pl.pallas_call(functools.partial(exchange_kernel, rows), out_shape=jax.Sh...  24.7 us
    pallas_call x1, Pallas kernels, shards(): pl.pallas_call(functools.partial(refine_kernel, pseudo), out_shape=jax.Sh...  7.12 us
    pallas_call x1, Pallas kernels, shards(): pl.pallas_call(gather_kernel, out_shape=jax.ShapeDtypeStruct((lanes,) + p...  6.71 us
    unnamed x12, local copies, waits for them, and re-layouts  3.01 us

profile of v3, /device:TPU:0, one launch (start us, length us, event | category | flops | bytes accessed | tf_op | source)
XLA Modules:
  0.0 76.2 jit_solution(17398606386615472961)
XLA Ops:
  0.6 0.0 copy-start.1
  0.6 1.0 %copy-done.1 = f32[4,128,256]{2,1,0:T(8,128)S(1)} copy-done((f32[4,128,256]{2,1,0:T(8,128)S(1)}, f32[4,128,256]{2,1,0:T(8,128)}, u32[]{:S(2)}) %copy-start.1) | copy-done | bytes 524312
  1.7 24.7 %exchange.1.img = f32[640,512]{1,0:T(8,128)S(1)} custom-call(f32[4,128,256]{2,1,0:T(8,128)S(1)} %copy-done.1), custom_call_target="tpu_custom_call" | custom-call | tf_op jit(solution)/shard_map/exchange/pallas_call | solution.py:390
  26.4 0.0 copy-start
  26.4 1.1 %copy-done = f32[640,512]{1,0:T(8,128)} copy-done((f32[640,512]{1,0:T(8,128)}, f32[640,512]{1,0:T(8,128)S(1)}, u32[]{:S(2)}) %copy-start) | copy-done | bytes 1310744
  27.5 0.0 copy-start.3
  27.5 0.0 copy-start.4
  27.5 0.0 copy-start.5
  27.5 34.0 %features.1 = (f32[20,1024]{1,0:T(8,128)}, f32[16,1024]{1,0:T(8,128)}) custom-call(f32[640,512]{1,0:T(8,128)} %copy-done, s32[32,16,256]{2,1,0:T(8,128)} %ids.1, f32[5,16]{1,0:T(8,128)} %bitcast.6, f32[5,16]{1,0:T(8,128)} %bitcast.7, f32[5,16]{1,0:T(8,128)} %bitcast.8, s32[1,1024]{1,0:T(1,128)} %bitcast.9), custom_call_target="tpu_custom_call" | custom-call | tf_op jit(solution)/shard_map/features/pallas_call | solution.py:412
  61.5 0.0 copy-start.2
  61.5 0.9 %copy-done.2 = f32[20,1024]{1,0:T(8,128)S(1)} copy-done((f32[20,1024]{1,0:T(8,128)S(1)}, f32[20,1024]{1,0:T(8,128)}, u32[]{:S(2)}) %copy-start.2) | copy-done | bytes 81944
  62.4 6.7 %gather.1.pay = f32[4,20,1024]{2,1,0:T(8,128)S(1)} custom-call(f32[20,1024]{1,0:T(8,128)S(1)} %copy-done.2), custom_call_target="tpu_custom_call" | custom-call | tf_op jit(solution)/shard_map/gather/pallas_call | solution.py:435
  69.1 0.0 copy-done.3
  69.1 0.0 copy-done.4
  69.1 0.0 copy-done.5
  69.1 7.1 %refine.1 = f32[16,128]{1,0:T(8,128)} custom-call(f32[4,20,1024]{2,1,0:T(8,128)S(1)} %gather.1.pay, f32[16,32]{1,0:T(8,128)S(1)} %copy-done.3, s32[1,128]{1,0:T(1,128)S(1)} %bitcast.5, f32[16,128]{1,0:T(8,128)S(1)} %copy-done.4), custom_call_target="tpu_custom_call" | custom-call | tf_op jit(solution)/shard_map/refine/pallas_call | solution.py:448
Async XLA Ops:
  0.6 1.0 %copy-start.1 = (f32[4,128,256]{2,1,0:T(8,128)S(1)}, f32[4,128,256]{2,1,0:T(8,128)}, u32[]{:S(2)}) copy-start(f32[4,128,256]{2,1,0:T(8,128)} %img.1) | copy-start | bytes 1572868
  26.4 1.1 %copy-start = (f32[640,512]{1,0:T(8,128)}, f32[640,512]{1,0:T(8,128)S(1)}, u32[]{:S(2)}) copy-start(f32[640,512]{1,0:T(8,128)S(1)} %exchange.1.img) | copy-start | bytes 3932164
  27.5 41.6 %copy-start.3 = (f32[16,32]{1,0:T(8,128)S(1)}, f32[16,32]{1,0:T(8,128)}, u32[]{:S(2)}) copy-start(f32[16,32]{1,0:T(8,128)} %coarse.1) | copy-start | bytes 6148
  27.5 41.6 %copy-start.4 = (f32[16,128]{1,0:T(8,128)S(1)}, f32[16,128]{1,0:T(8,128)}, u32[]{:S(2)}) copy-start(f32[16,128]{1,0:T(8,128)} %offsets.1) | copy-start | bytes 24580
  27.5 41.6 %copy-start.5 = (s32[128]{0:T(128)S(1)}, s32[128]{0:T(128)}, u32[]{:S(2)}) copy-start(s32[128]{0:T(128)} %param.16) | copy-start | bytes 1540
  61.5 0.9 %copy-start.2 = (f32[20,1024]{1,0:T(8,128)S(1)}, f32[20,1024]{1,0:T(8,128)}, u32[]{:S(2)}) copy-start(f32[20,1024]{1,0:T(8,128)} %get-tuple-element.5.pay) | copy-start | bytes 245764

commit v4 on v3

--- a/solution.py
+++ b/solution.py
@@ -105,9 +105,9 @@
         )
 
     def start(d, carry):
-        j = lax.rem(here + lax.rem(d + stacks // 2, stacks), stacks)
-
-        @pl.when(j != here)
+        j = lax.rem(here + d, stacks)
+
+        @pl.when(d > 0)
         def _():
             main_copy(j, here).start()
 
@@ -409,6 +409,7 @@
     )(slab_image)
     highs = fragments // LO
     assert highs <= 16
+    grant = (16 << 20) + 144 * depth * rows * cols
     pay, means = pl.pallas_call(
         feature_kernel,
         out_shape=(
@@ -429,7 +430,7 @@
             pltpu.VMEM((highs * chans + 16, ROWS * cols), BF16),
             pltpu.VMEM((LO, ROWS * cols), BF16),
         ],
-        compiler_params=pltpu.CompilerParams(vmem_limit_bytes=56 << 20),
+        compiler_params=pltpu.CompilerParams(vmem_limit_bytes=grant),
         name="features",
     )(pencil, fragment_ids, width_taps.T, height_taps.T, depth_taps.T, fragment_owner.reshape(1, fragments))
     gathered = pl.pallas_call(
@@ -439,7 +440,7 @@
         out_specs=pl.BlockSpec(memory_space=pltpu.VMEM),
         scratch_shapes=[pltpu.SemaphoreType.DMA((lanes,)), pltpu.SemaphoreType.DMA((lanes,))],
         compiler_params=pltpu.CompilerParams(
-            collective_id=1, has_side_effects=True, vmem_limit_bytes=32 << 20
+            collective_id=1, has_side_effects=True, vmem_limit_bytes=16 << 20
         ),
         name="gather",
     )(pay)

time: 76.5 us -> 71.3 us (0.932)
  the two profiles are of different devices: /device:TPU:0 before, /device:TPU:25 now
where the time goes in v4:
time: 71.3 us; the launch traced here: 71.2 us
  Pallas kernels  69.3 us (97%)
  local copies, waits for them, and re-layouts  1.08 us (2%)
  between operations  0.76 us (1%)
    pallas_call x1, Pallas kernels, shards(): pl.pallas_call(feature_kernel, out_shape=(jax.ShapeDtypeStruct((chans + l...  32.4 us
    pallas_call x1, Pallas kernels, shards(): pl.pallas_call(functools.partial(exchange_kernel, rows), out_shape=jax.Sh...  22.3 us
    pallas_call x1, Pallas kernels, shards(): pl.pallas_call(gather_kernel, out_shape=jax.ShapeDtypeStruct((lanes,) + p...  7.55 us
    pallas_call x1, Pallas kernels, shards(): pl.pallas_call(functools.partial(refine_kernel, pseudo), out_shape=jax.Sh...  7.12 us

profile of v4, /device:TPU:25, one launch (start us, length us, event | category | flops | bytes accessed | tf_op | source)
XLA Modules:
  0.0 71.2 jit_solution(8847181688747220528)
XLA Ops:
  0.6 0.0 copy-start.5
  0.6 0.0 copy-start.4
  0.7 0.0 copy-start
  0.7 1.0 %copy-done = f32[4,128,256]{2,1,0:T(8,128)S(1)} copy-done((f32[4,128,256]{2,1,0:T(8,128)S(1)}, f32[4,128,256]{2,1,0:T(8,128)}, u32[]{:S(2)}) %copy-start) | copy-done | bytes 524312
  1.7 0.0 copy-start.1
  1.7 0.0 copy-start.6
  1.7 0.0 copy-start.7
  1.7 22.3 %exchange.1.img = f32[640,512]{1,0:T(8,128)S(1)} custom-call(f32[4,128,256]{2,1,0:T(8,128)S(1)} %copy-done), custom_call_target="tpu_custom_call" | custom-call | tf_op jit(solution)/shard_map/exchange/pallas_call | solution.py:390
  24.0 0.0 copy-done.5
  24.0 0.0 copy-done.4
  24.0 0.0 copy-done.1
  24.0 0.0 copy-done.6
  24.1 0.0 copy-done.7
  24.1 0.0 copy-start.2
  24.1 0.0 copy-start.3
  24.1 0.0 copy-start.8
  24.1 32.4 %features.1 = (f32[20,1024]{1,0:T(8,128)S(1)}, f32[16,1024]{1,0:T(8,128)}) custom-call(f32[640,512]{1,0:T(8,128)S(1)} %exchange.1.img, s32[32,16,256]{2,1,0:T(8,128)S(1)} %copy-done.1, f32[5,16]{1,0:T(8,128)S(1)} %bitcast.5, f32[5,16]{1,0:T(8,128)S(1)} %bitcast.6, f32[5,16]{1,0:T(8,128)S(1)} %bitcast.7, s32[1,1024]{1,0:T(1,128)S(1)} %bitcast.8), custom_call_target="tpu_custom_call" | custom-call | tf_op jit(solution)/shard_map/features/pallas_call | solution.py:413
  56.5 7.6 %gather.1.pay = f32[4,20,1024]{2,1,0:T(8,128)S(1)} custom-call(f32[20,1024]{1,0:T(8,128)S(1)} %get-tuple-element.5.pay), custom_call_target="tpu_custom_call" | custom-call | tf_op jit(solution)/shard_map/gather/pallas_call | solution.py:436
  64.0 0.0 copy-done.2
  64.0 0.0 copy-done.3
  64.1 0.0 copy-done.8
  64.1 7.1 %refine.1 = f32[16,128]{1,0:T(8,128)} custom-call(f32[4,20,1024]{2,1,0:T(8,128)S(1)} %gather.1.pay, f32[16,32]{1,0:T(8,128)S(1)} %copy-done.2, s32[1,128]{1,0:T(1,128)S(1)} %bitcast.9, f32[16,128]{1,0:T(8,128)S(1)} %copy-done.3), custom_call_target="tpu_custom_call" | custom-call | tf_op jit(solution)/shard_map/refine/pallas_call | solution.py:449
Async XLA Ops:
  0.6 23.4 %copy-start.5 = (f32[16,5]{0,1:T(8,128)S(1)}, f32[16,5]{0,1:T(8,128)}, u32[]{:S(2)}) copy-start(f32[16,5]{0,1:T(8,128)} %param.11) | copy-start | bytes 964
  0.6 23.4 %copy-start.4 = (f32[16,5]{0,1:T(8,128)S(1)}, f32[16,5]{0,1:T(8,128)}, u32[]{:S(2)}) copy-start(f32[16,5]{0,1:T(8,128)} %param.10) | copy-start | bytes 964
  0.7 1.1 %copy-start = (f32[4,128,256]{2,1,0:T(8,128)S(1)}, f32[4,128,256]{2,1,0:T(8,128)}, u32[]{:S(2)}) copy-start(f32[4,128,256]{2,1,0:T(8,128)} %img.1) | copy-start | bytes 1572868
  1.7 22.3 %copy-start.1 = (s32[32,16,256]{2,1,0:T(8,128)S(1)}, s32[32,16,256]{2,1,0:T(8,128)}, u32[]{:S(2)}) copy-start(s32[32,16,256]{2,1,0:T(8,128)} %ids.1) | copy-start | bytes 1572868
  1.7 22.3 %copy-start.6 = (f32[16,5]{0,1:T(8,128)S(1)}, f32[16,5]{0,1:T(8,128)}, u32[]{:S(2)}) copy-start(f32[16,5]{0,1:T(8,128)} %param.12) | copy-start | bytes 964
  1.7 22.3 %copy-start.7 = (s32[1024,1]{0,1:T(1,128)S(1)}, s32[1024,1]{0,1:T(1,128)}, u32[]{:S(2)}) copy-start(s32[1024,1]{0,1:T(1,128)} %param.14) | copy-start | bytes 12292
  24.1 40.0 %copy-start.2 = (f32[16,32]{1,0:T(8,128)S(1)}, f32[16,32]{1,0:T(8,128)}, u32[]{:S(2)}) copy-start(f32[16,32]{1,0:T(8,128)} %coarse.1) | copy-start | bytes 6148
  24.1 40.0 %copy-start.3 = (f32[16,128]{1,0:T(8,128)S(1)}, f32[16,128]{1,0:T(8,128)}, u32[]{:S(2)}) copy-start(f32[16,128]{1,0:T(8,128)} %offsets.1) | copy-start | bytes 24580
  24.1 40.0 %copy-start.8 = (s32[128]{0:T(128)S(1)}, s32[128]{0:T(128)}, u32[]{:S(2)}) copy-start(s32[128]{0:T(128)} %param.16) | copy-start | bytes 1540
